TPU v7x, 256 devices: a whole 4x4x8 slice. The times are simulated.
256 devices in a mesh: dp: 2 (over core), row: 16 (over x, y), col: 8 (over z).
Axes of the slice: x: 4, y: 4, z: 8, core: 2. Of those that a mesh axis runs over, the one named last changes fastest.
Arguments:
- tokens: bfloat16 [1536, 8192], P('dp', 'row'), may hold values from -6 to 6
- out_grad: bfloat16 [1536, 8192], P('dp', 'row'), may hold values from -6 to 6
- gate_weight: bfloat16 [8192, 14336], P('row', 'col'), may hold values from -0.0625 to 0.0625
- up_weight: bfloat16 [8192, 14336], P('row', 'col'), may hold values from -0.0625 to 0.0625
- down_weight: bfloat16 [14336, 8192], P('col', 'row'), may hold values from -0.046875 to 0.046875
- gate_mask: int32 [64, 112], P('row', 'col'), may hold values from 0 to 1, as said below
- up_mask: int32 [64, 112], P('row', 'col'), may hold values from 0 to 1, as said below
- down_mask: int32 [112, 64], P('col', 'row'), may hold values from 0 to 1, as said below
Outputs:
- output: bfloat16 [1536, 8192], P(('dp', 'col'), 'row')
- token_grad: bfloat16 [1536, 8192], P(('dp', 'col'), 'row')
- gate_grad: bfloat16 [8192, 14336], P('row', 'col')
- up_grad: bfloat16 [8192, 14336], P('row', 'col')
- down_grad: bfloat16 [14336, 8192], P('col', 'row')
Inputs may be any that keep to these rules, and one draw needn't show every extreme that they name: `gate_mask`: one keep flag for each 128 x 128 block of the matrix; the share kept differs from block row to block row. `up_mask`: one keep flag for each 128 x 128 block of the matrix; the share kept differs from block row to block row. `down_mask`: one keep flag for each 128 x 128 block of the matrix; the share kept differs from block column to block column.
All inputs are finite; a program needn't handle non-finite values.
Results may differ from a plain program's by a relative error of at most 0.029.
Values may be sent and summed in bfloat16 or wider, within the bound.
A program may use at most 128 MiB of HBM per device.

v0:
```python
import jax
import jax.numpy as jnp
from jax import lax
from jax.sharding import PartitionSpec as P

BLOCK = 128


def expand(mask_tile):
    return jnp.repeat(jnp.repeat(mask_tile, BLOCK, axis=0), BLOCK, axis=1)


def contract_rows(left_side, right_side):
    return lax.dot_general(
        left_side, right_side, (((0,), (0,)), ((), ())), preferred_element_type=jnp.float32
    )


def contract_cols(left_side, right_side):
    return lax.dot_general(
        left_side, right_side, (((1,), (1,)), ((), ())), preferred_element_type=jnp.float32
    )


def body(tokens, out_grad, gate_weight, up_weight, down_weight, gate_mask, up_mask, down_mask):
    gate_keep = expand(gate_mask)
    up_keep = expand(up_mask)
    down_keep = expand(down_mask)
    gate_eff = gate_weight * gate_keep.astype(jnp.bfloat16)
    up_eff = up_weight * up_keep.astype(jnp.bfloat16)
    down_eff = down_weight * down_keep.astype(jnp.bfloat16)
    gate_part = jnp.dot(tokens, gate_eff, preferred_element_type=jnp.float32)
    up_part = jnp.dot(tokens, up_eff, preferred_element_type=jnp.float32)
    gate_share, up_share = (
        lax.psum_scatter(
            gate_part.astype(jnp.bfloat16), "row", scatter_dimension=0, tiled=True
        ).astype(jnp.float32),
        lax.psum_scatter(
            up_part.astype(jnp.bfloat16), "row", scatter_dimension=0, tiled=True
        ).astype(jnp.float32),
    )
    gate_sig = jax.nn.sigmoid(gate_share)
    silu_gate = gate_share * gate_sig
    hidden_share = (silu_gate * up_share).astype(jnp.bfloat16)
    hidden = lax.all_gather(hidden_share, "row", axis=0, tiled=True)
    output = lax.psum_scatter(
        jnp.dot(hidden, down_eff, preferred_element_type=jnp.float32).astype(jnp.bfloat16),
        "col",
        scatter_dimension=0,
        tiled=True,
    )
    down_local = contract_rows(hidden, out_grad) * down_keep.astype(jnp.float32)
    back_part = contract_cols(out_grad, down_eff)
    back_share = lax.psum_scatter(
        back_part.astype(jnp.bfloat16), "row", scatter_dimension=0, tiled=True
    ).astype(jnp.float32)
    gate_deriv = (back_share * up_share * gate_sig * (1.0 + gate_share * (1.0 - gate_sig))).astype(
        jnp.bfloat16
    )
    up_deriv = (back_share * silu_gate).astype(jnp.bfloat16)
    gate_full, up_full = (
        lax.all_gather(gate_deriv, "row", axis=0, tiled=True),
        lax.all_gather(up_deriv, "row", axis=0, tiled=True),
    )
    token_grad = lax.psum_scatter(
        (contract_cols(gate_full, gate_eff) + contract_cols(up_full, up_eff)).astype(jnp.bfloat16),
        "col",
        scatter_dimension=0,
        tiled=True,
    )
    gate_local = contract_rows(tokens, gate_full) * gate_keep.astype(jnp.float32)
    up_local = contract_rows(tokens, up_full) * up_keep.astype(jnp.float32)
    gate_total, up_total, down_total = (
        lax.psum(gate_local.astype(jnp.bfloat16), "dp").astype(jnp.float32),
        lax.psum(up_local.astype(jnp.bfloat16), "dp").astype(jnp.float32),
        lax.psum(down_local.astype(jnp.bfloat16), "dp").astype(jnp.float32),
    )
    return (
        output,
        token_grad,
        gate_total.astype(jnp.bfloat16),
        up_total.astype(jnp.bfloat16),
        down_total.astype(jnp.bfloat16),
    )


def solution(mesh):
    placed = (
        P("dp", "row"),
        P("dp", "row"),
        P("row", "col"),
        P("row", "col"),
        P("col", "row"),
        P("row", "col"),
        P("row", "col"),
        P("col", "row"),
    )
    return jax.shard_map(
        body,
        mesh=mesh,
        in_specs=placed,
        out_specs=(
            P(("dp", "col"), "row"),
            P(("dp", "col"), "row"),
            P("row", "col"),
            P("row", "col"),
            P("col", "row"),
        ),
        check_vma=False,
    )
```

profile of v0, /device:TPU:2, one launch (start us, length us, event | category | flops | bytes accessed | tf_op | source)
XLA Modules:
  0.0 568.2 jit_solution(9316289985637627538)
XLA Ops:
  8.2 5.1 broadcast_in_dim.35
  13.3 1.2 copy-done.8
  14.5 1.6 fusion.5
  16.2 2.9 copy.59
  19.1 2.8 copy.43
  22.3 1.2 copy-done.4
  23.6 1.6 fusion.3
  25.2 2.9 copy.55
  28.2 2.8 copy.46
  31.4 1.2 copy-done.5
  32.6 1.6 fusion.4
  34.2 2.9 copy.57
  37.2 66.0 %reduce-scatter.20.cloned.1.call-done = bf16[48,1792]{1,0:T(8,128)(2,1)} async-done(((bf16[768,1792]{1,0:T(8,128)(2,1)}), bf16[48,1792]{1,0:T(8,128)(2,1)}) %reduce-scatter.20.cloned.1.call-update) | async-done | bytes 172048 | tf_op jit(solution)/shard_map/reduce_scatter | solution.py:54
  103.2 84.2 %reduce-scatter.16.cloned.1.call-done = bf16[48,1792]{1,0:T(8,128)(2,1)} async-done(((bf16[768,1792]{1,0:T(8,128)(2,1)}), bf16[48,1792]{1,0:T(8,128)(2,1)}) %reduce-scatter.16.cloned.1.call-update) | async-done | bytes 172048 | tf_op jit(solution)/shard_map/reduce_scatter | solution.py:35
  187.5 84.3 %reduce-scatter.18.cloned.1.call-done = bf16[48,1792]{1,0:T(8,128)(2,1)} async-done(((bf16[768,1792]{1,0:T(8,128)(2,1)}), bf16[48,1792]{1,0:T(8,128)(2,1)}) %reduce-scatter.18.cloned.1.call-update) | async-done | bytes 172048 | tf_op jit(solution)/shard_map/reduce_scatter | solution.py:38
  271.7 2.1 fusion.10
  275.7 48.8 %all-gather.6.cloned.1.call-done = bf16[768,1792]{1,0:T(8,128)(2,1)} async-done(((bf16[48,1792]{1,0:T(8,128)(2,1)}), bf16[768,1792]{1,0:T(8,128)(2,1)}) %all-gather.6.cloned.1.call-update) | async-done | bytes 2752528 | tf_op jit(solution)/shard_map/all_gather | solution.py:62
  324.5 4.7 fusion.2
  329.2 48.4 %all-gather.8.cloned.1.call-done = bf16[768,1792]{1,0:T(8,128)(2,1)} async-done(((bf16[48,1792]{1,0:T(8,128)(2,1)}), bf16[768,1792]{1,0:T(8,128)(2,1)}) %all-gather.8.cloned.1.call-update) | async-done | bytes 2752528 | tf_op jit(solution)/shard_map/all_gather | solution.py:63
  377.6 4.7 fusion.1
  382.3 48.4 %all-gather.4.cloned.1.call-done = bf16[768,1792]{1,0:T(8,128)(2,1)} async-done(((bf16[48,1792]{1,0:T(8,128)(2,1)}), bf16[768,1792]{1,0:T(8,128)(2,1)}) %all-gather.4.cloned.1.call-update) | async-done | bytes 2752528 | tf_op jit(solution)/shard_map/all_gather | solution.py:45
  430.8 2.2 broadcast_in_dim.41
  433.0 2.9 fusion
  436.0 5.5 convolution_convert_fusion.3
  441.6 3.2 fusion.18
  444.8 2.5 add_convert_fusion
  447.3 29.8 %all-reduce.3.cloned.1.call-done = (bf16[512,1792]{0,1:T(8,128)(2,1)}, bf16[512,1792]{0,1:T(8,128)(2,1)}, bf16[1792,512]{1,0:T(8,128)(2,1)}) async-done(((bf16[512,1792]{0,1:T(8,128)(2,1)}, bf16[512,1792]{0,1:T(8,128)(2,1)}, bf16[1792,512]{1,0:T(8,128)(2,1)}), (bf16[512,1792]{0,1:T(8,128)(2,1)}, bf16[512,1792]{0,1:T(8,128)(2,1)}, bf16[1792,512]{1,0:T(8,128)(2,1)})) %all-reduce.3.cloned.1.call-update) | async-done | bytes 5505040 | tf_op jit(solution)/shard_map/psum | solution.py:74
  477.1 3.8 copy.53
  480.9 3.9 copy.54
  484.8 35.0 %reduce-scatter.12.cloned.1.call-done = bf16[96,512]{1,0:T(8,128)(2,1)} async-done(((bf16[768,512]{1,0:T(8,128)(2,1)}), bf16[96,512]{1,0:T(8,128)(2,1)}) %reduce-scatter.12.cloned.1.call-update) | async-done | bytes 98320 | tf_op jit(solution)/shard_map/reduce_scatter | solution.py:46
  519.9 40.1 %reduce-scatter.14.cloned.1.call-done = bf16[96,512]{1,0:T(8,128)(2,1)} async-done(((bf16[768,512]{1,0:T(8,128)(2,1)}), bf16[96,512]{1,0:T(8,128)(2,1)}) %reduce-scatter.14.cloned.1.call-update) | async-done | bytes 98320 | tf_op jit(solution)/shard_map/reduce_scatter | solution.py:65
  560.0 1.2 copy.74
  (70 shorter events, 4.4 us)
Async XLA Ops:
  7.2 16.4 %copy-start = (bf16[768,512]{1,0:T(8,128)(2,1)S(1)}, bf16[768,512]{1,0:T(8,128)(2,1)}, u32[]{:S(2)}) copy-start(bf16[768,512]{1,0:T(8,128)(2,1)} %param.8) | copy-start | bytes 2359300
  7.2 96.1 %reduce-scatter.20.cloned.1.call-start = ((), (), s32[]{:S(2)}) async-start(), calls=%async_computation.12 | async-start | bytes 2924544 | tf_op jit(solution)/shard_map/reduce_scatter | solution.py:54
  8.1 6.4 %copy-start.12 = (bf16[1792,512]{1,0:T(8,128)(2,1)S(1)}, bf16[1792,512]{1,0:T(8,128)(2,1)}, u32[]{:S(2)}) copy-start(bf16[1792,512]{1,0:T(8,128)(2,1)} %param.12) | copy-start | bytes 5505028
  8.1 6.4 %copy-start.13 = (bf16[768,512]{1,0:T(8,128)(2,1)S(1)}, bf16[768,512]{1,0:T(8,128)(2,1)}, u32[]{:S(2)}) copy-start(bf16[768,512]{1,0:T(8,128)(2,1)} %param.9) | copy-start | bytes 2359300
  13.3 1.2 copy-start.8
  19.1 2.9 copy-start.9
  19.1 168.4 %reduce-scatter.16.cloned.1.call-start = ((), (), s32[]{:S(2)}) async-start(), calls=%async_computation.10 | async-start | bytes 2924544 | tf_op jit(solution)/shard_map/reduce_scatter | solution.py:35
  22.3 1.2 copy-start.4
  28.1 2.9 copy-start.10
  28.1 243.6 %reduce-scatter.18.cloned.1.call-start = ((), (), s32[]{:S(2)}) async-start(), calls=%async_computation.11 | async-start | bytes 2924544 | tf_op jit(solution)/shard_map/reduce_scatter | solution.py:38
  31.4 1.2 copy-start.5
  37.2 287.3 %all-gather.6.cloned.1.call-start = ((), (), s32[]{:S(2)}) async-start(), calls=%async_computation.7 | async-start | bytes 2924544 | tf_op jit(solution)/shard_map/all_gather | solution.py:62
  273.8 103.8 %all-gather.8.cloned.1.call-start = ((), (), s32[]{:S(2)}) async-start(), calls=%async_computation.8 | async-start | bytes 2924544 | tf_op jit(solution)/shard_map/all_gather | solution.py:63
  274.4 156.3 %all-gather.4.cloned.1.call-start = ((), (), s32[]{:S(2)}) async-start(), calls=%async_computation.5 | async-start | bytes 2924544 | tf_op jit(solution)/shard_map/all_gather | solution.py:45
  275.0 202.1 %all-reduce.3.cloned.1.call-start = ((), (), s32[]{:S(2)}) async-start(), calls=%async_computation.13 | async-start | bytes 11010048 | tf_op jit(solution)/shard_map/psum | solution.py:74
  430.7 2.2 copy-start.11
  430.8 2.2 copy-start.14
  435.9 5.7 copy-start.2
  435.9 83.9 %reduce-scatter.12.cloned.1.call-start = ((), (), s32[]{:S(2)}) async-start(), calls=%async_computation.6 | async-start | bytes 884736 | tf_op jit(solution)/shard_map/reduce_scatter | solution.py:46
  441.5 118.5 %reduce-scatter.14.cloned.1.call-start = ((), (), s32[]{:S(2)}) async-start(), calls=%async_computation.9 | async-start | bytes 884736 | tf_op jit(solution)/shard_map/reduce_scatter | solution.py:65
  441.6 3.3 copy-start.3
  441.6 3.3 copy-start.6
  480.9 79.1 %copy-start.7 = (bf16[1792,512]{1,0:T(8,128)(2,1)S(1)}, bf16[1792,512]{1,0:T(8,128)(2,1)}, u32[]{:S(2)}) copy-start(bf16[1792,512]{1,0:T(8,128)(2,1)} %get-tuple-element.41) | copy-start | bytes 5505028
  560.0 1.7 copy-start.1
Sparse Core Ops, SparseCore 0:
  19.2 84.0 reduce-scatter.19
  106.8 80.5 reduce-scatter.15
  191.1 80.5 reduce-scatter.17
  274.1 50.4 all-gather.5
  326.9 50.6 all-gather.7
  379.9 50.6 all-gather.3
  436.0 41.0 all-reduce.2
  480.2 39.6 reduce-scatter.11
  523.0 36.9 reduce-scatter.13
where the time goes:
time: 569 us; the launch traced here: 568 us
  waiting for transfers between devices  486 us (85%)
  local copies, waits for them, and re-layouts  35.8 us (6%)
  matrix products  28.4 us (5%)
  between operations  14.2 us (2%)
    reduce_scatter x1, waiting for transfers between devices, body(): lax.psum_scatter(up_part.astype(jnp.bfloat16), 'row', scatter_dimension=0...  84.3 us
    reduce_scatter x1, waiting for transfers between devices, body(): lax.psum_scatter(gate_part.astype(jnp.bfloat16), 'row', scatter_dimension...  84.2 us
    reduce_scatter x1, waiting for transfers between devices, body(): lax.psum_scatter(back_part.astype(jnp.bfloat16), 'row', scatter_dimension...  66 us
    all_gather x1, waiting for transfers between devices, body(): lax.all_gather(gate_deriv, 'row', axis=0, tiled=True)  48.8 us
    all_gather x1, waiting for transfers between devices, body(): hidden = lax.all_gather(hidden_share, 'row', axis=0, tiled=True)  48.4 us
    all_gather x1, waiting for transfers between devices, body(): lax.all_gather(up_deriv, 'row', axis=0, tiled=True)  48.4 us
    reduce_scatter x1, waiting for transfers between devices, body(): lax.psum_scatter((contract_cols(gate_full, gate_eff) + contract_cols(up_f...  40.1 us
    reduce_scatter x1, waiting for transfers between devices, body(): lax.psum_scatter(jnp.dot(hidden, down_eff, preferred_element_type=jnp.flo...  35 us
  transfers between devices with their start and end apart: 9, of which 9 were waited for; matrix products, arithmetic and copies ran while one was open for 8% of the time, Pallas kernels for 0%

commit v1 on v0

--- a/solution.py
+++ b/solution.py
@@ -59,7 +59,9 @@
     )
     up_deriv = (back_share * silu_gate).astype(jnp.bfloat16)
     gate_full, up_full = (
-        lax.all_gather(gate_deriv, "row", axis=0, tiled=True),
+        jnp.concatenate(
+            lax.all_to_all(jnp.stack([gate_deriv] * lax.axis_size("row")), "row", 0, 0), axis=0
+        ),
         lax.all_gather(up_deriv, "row", axis=0, tiled=True),
     )
     token_grad = lax.psum_scatter(

time: 569 us -> 538 us (0.946)
  waiting for transfers between devices: 486 us -> 446 us
    all_gather x1 -> x0, waiting for transfers between devices: 48.8 us -> none  [body(): lax.all_gather(gate_deriv, 'row', axis=0, tiled=True)]
    all_to_all x0 -> x1, waiting for transfers between devices: none -> 32.9 us  [body(): lax.all_to_all(jnp.stack([gate_deriv] * lax.axis_size('row')), 'row', 0, 0)]
    all_gather x1, waiting for transfers between devices: 48.4 us -> 24.9 us  [body(): lax.all_gather(up_deriv, 'row', axis=0, tiled=True)]
    unnamed x50 -> x48, local copies, waits for them, and re-layouts: 27.8 us -> 29 us
  transfers between devices with their start and end apart: 9 -> 9, of which waited for: 9 -> 9; matrix products, arithmetic and copies ran while one was open for 8% -> 9% of each run, Pallas kernels for 0% -> 0%
where the time goes in v1:
time: 538 us; the launch traced here: 537 us
  waiting for transfers between devices  446 us (83%)
  local copies, waits for them, and re-layouts  39.4 us (7%)
  matrix products  27.1 us (5%)
  between operations  14.4 us (3%)
  starting transfers between devices  6.17 us (1%)
    reduce_scatter x1, waiting for transfers between devices, body(): lax.psum_scatter(up_part.astype(jnp.bfloat16), 'row', scatter_dimension=0...  84.4 us
    reduce_scatter x1, waiting for transfers between devices, body(): lax.psum_scatter(gate_part.astype(jnp.bfloat16), 'row', scatter_dimension...  84.4 us
    reduce_scatter x1, waiting for transfers between devices, body(): lax.psum_scatter(back_part.astype(jnp.bfloat16), 'row', scatter_dimension...  65.5 us
    all_gather x1, waiting for transfers between devices, body(): hidden = lax.all_gather(hidden_share, 'row', axis=0, tiled=True)  48.4 us
    reduce_scatter x1, waiting for transfers between devices, body(): lax.psum_scatter((contract_cols(gate_full, gate_eff) + contract_cols(up_f...  40.1 us
    reduce_scatter x1, waiting for transfers between devices, body(): lax.psum_scatter(jnp.dot(hidden, down_eff, preferred_element_type=jnp.flo...  35 us
    all_to_all x1, waiting for transfers between devices, body(): lax.all_to_all(jnp.stack([gate_deriv] * lax.axis_size('row')), 'row', 0, 0)  32.9 us
    psum x1, waiting for transfers between devices, body(): lax.psum(gate_local.astype(jnp.bfloat16), 'dp').astype(jnp.float32)  29.9 us
  transfers between devices with their start and end apart: 9, of which 9 were waited for; matrix products, arithmetic and copies ran while one was open for 9% of the time, Pallas kernels for 0%

profile of v1, /device:TPU:2, one launch (start us, length us, event | category | flops | bytes accessed | tf_op | source)
XLA Modules:
  0.0 537.1 jit_solution(3253094477257127090)
XLA Ops:
  8.2 5.1 broadcast_in_dim.35
  13.3 1.2 copy-done.7
  14.5 1.6 fusion.5
  16.2 2.9 copy.61
  19.1 2.8 copy.45
  23.6 1.6 fusion.3
  25.2 2.9 copy.57
  28.2 2.8 copy.48
  33.2 1.6 fusion.4
  34.8 2.8 copy.59
  37.7 65.5 %reduce-scatter.20.cloned.1.call-done = bf16[48,1792]{1,0:T(8,128)(2,1)} async-done(((bf16[768,1792]{1,0:T(8,128)(2,1)}), bf16[48,1792]{1,0:T(8,128)(2,1)}) %reduce-scatter.20.cloned.1.call-update) | async-done | bytes 172048 | tf_op jit(solution)/shard_map/reduce_scatter | solution.py:54
  103.3 84.4 %reduce-scatter.16.cloned.1.call-done = bf16[48,1792]{1,0:T(8,128)(2,1)} async-done(((bf16[768,1792]{1,0:T(8,128)(2,1)}), bf16[48,1792]{1,0:T(8,128)(2,1)}) %reduce-scatter.16.cloned.1.call-update) | async-done | bytes 172048 | tf_op jit(solution)/shard_map/reduce_scatter | solution.py:35
  187.7 84.4 %reduce-scatter.18.cloned.1.call-done = bf16[48,1792]{1,0:T(8,128)(2,1)} async-done(((bf16[768,1792]{1,0:T(8,128)(2,1)}), bf16[48,1792]{1,0:T(8,128)(2,1)}) %reduce-scatter.18.cloned.1.call-update) | async-done | bytes 172048 | tf_op jit(solution)/shard_map/reduce_scatter | solution.py:38
  272.1 2.1 fusion.10
  274.8 1.7 stack.2
  276.5 5.7 %all-to-all-start = ((bf16[16,48,1792]{2,1,0:T(8,128)(2,1)}), bf16[16,48,1792]{2,1,0:T(8,128)(2,1)S(1)}, u32[]{:S(2)}, u32[]{:S(2)}) async-start(bf16[16,48,1792]{2,1,0:T(8,128)(2,1)} %stack.2), calls=%async_computation.1 | async-start | bytes 5505024 | tf_op jit(solution)/shard_map/all_to_all | solution.py:63
  284.8 32.9 %all-to-all-done = bf16[16,48,1792]{2,1,0:T(8,128)(2,1)S(1)} async-done(((bf16[16,48,1792]{2,1,0:T(8,128)(2,1)}), bf16[16,48,1792]{2,1,0:T(8,128)(2,1)S(1)}, u32[]{:S(2)}, u32[]{:S(2)}) %all-to-all-start) | async-done | bytes 2752544 | tf_op jit(solution)/shard_map/all_to_all | solution.py:63
  317.7 3.6 fusion.2
  321.3 24.9 %all-gather.5.cloned.1.call-done = bf16[768,1792]{1,0:T(8,128)(2,1)} async-done(((bf16[48,1792]{1,0:T(8,128)(2,1)}), bf16[768,1792]{1,0:T(8,128)(2,1)}) %all-gather.5.cloned.1.call-update) | async-done | bytes 2752528 | tf_op jit(solution)/shard_map/all_gather | solution.py:65
  346.3 4.6 fusion.1
  350.9 48.4 %all-gather.3.cloned.1.call-done = bf16[768,1792]{1,0:T(8,128)(2,1)} async-done(((bf16[48,1792]{1,0:T(8,128)(2,1)}), bf16[768,1792]{1,0:T(8,128)(2,1)}) %all-gather.3.cloned.1.call-update) | async-done | bytes 2752528 | tf_op jit(solution)/shard_map/all_gather | solution.py:45
  399.4 2.2 broadcast_in_dim.41
  401.6 2.9 fusion
  404.6 5.4 %convolution_convert_fusion.3 = bf16[768,512]{1,0:T(8,128)(2,1)} fusion(bf16[768,1792]{1,0:T(8,128)(2,1)} %all-gather.3.cloned.1.call-done, bf16[1792,512]{1,0:T(8,128)(2,1)} %param.12, bf16[224,8,4,128]{3,2,1,0:T(4,128)(2,1)} %bitcast.83), kind=kOutput, calls=%fused_computation.16 | convolution fusion | flops 1410596864 | bytes 7208960 | tf_op jit(solution)/shard_map/dot_general | solution.py:47
  410.0 3.2 fusion.18
  413.3 2.5 add_convert_fusion
  415.8 29.9 %all-reduce.3.cloned.1.call-done = (bf16[512,1792]{0,1:T(8,128)(2,1)}, bf16[512,1792]{0,1:T(8,128)(2,1)}, bf16[1792,512]{1,0:T(8,128)(2,1)}) async-done(((bf16[512,1792]{0,1:T(8,128)(2,1)}, bf16[512,1792]{0,1:T(8,128)(2,1)}, bf16[1792,512]{1,0:T(8,128)(2,1)}), (bf16[512,1792]{0,1:T(8,128)(2,1)}, bf16[512,1792]{0,1:T(8,128)(2,1)}, bf16[1792,512]{1,0:T(8,128)(2,1)})) %all-reduce.3.cloned.1.call-update) | async-done | bytes 5505040 | tf_op jit(solution)/shard_map/psum | solution.py:76
  445.7 3.8 copy.55
  449.5 3.9 copy.56
  453.4 35.0 %reduce-scatter.12.cloned.1.call-done = bf16[96,512]{1,0:T(8,128)(2,1)} async-done(((bf16[768,512]{1,0:T(8,128)(2,1)}), bf16[96,512]{1,0:T(8,128)(2,1)}) %reduce-scatter.12.cloned.1.call-update) | async-done | bytes 98320 | tf_op jit(solution)/shard_map/reduce_scatter | solution.py:46
  488.5 40.1 %reduce-scatter.14.cloned.1.call-done = bf16[96,512]{1,0:T(8,128)(2,1)} async-done(((bf16[768,512]{1,0:T(8,128)(2,1)}), bf16[96,512]{1,0:T(8,128)(2,1)}) %reduce-scatter.14.cloned.1.call-update) | async-done | bytes 98320 | tf_op jit(solution)/shard_map/reduce_scatter | solution.py:67
  528.6 1.2 copy.76
  (68 shorter events, 8.7 us)
Async XLA Ops:
  7.2 16.4 %copy-start = (bf16[768,512]{1,0:T(8,128)(2,1)S(1)}, bf16[768,512]{1,0:T(8,128)(2,1)}, u32[]{:S(2)}) copy-start(bf16[768,512]{1,0:T(8,128)(2,1)} %param.8) | copy-start | bytes 2359300
  7.2 96.1 %reduce-scatter.20.cloned.1.call-start = ((), (), s32[]{:S(2)}) async-start(), calls=%async_computation.12 | async-start | bytes 2924544 | tf_op jit(solution)/shard_map/reduce_scatter | solution.py:54
  8.1 6.4 %copy-start.11 = (bf16[1792,512]{1,0:T(8,128)(2,1)S(1)}, bf16[1792,512]{1,0:T(8,128)(2,1)}, u32[]{:S(2)}) copy-start(bf16[1792,512]{1,0:T(8,128)(2,1)} %param.12) | copy-start | bytes 5505028
  8.1 6.4 %copy-start.12 = (bf16[768,512]{1,0:T(8,128)(2,1)S(1)}, bf16[768,512]{1,0:T(8,128)(2,1)}, u32[]{:S(2)}) copy-start(bf16[768,512]{1,0:T(8,128)(2,1)} %param.9) | copy-start | bytes 2359300
  13.3 1.2 copy-start.7
  19.1 2.9 copy-start.8
  19.1 168.6 %reduce-scatter.16.cloned.1.call-start = ((), (), s32[]{:S(2)}) async-start(), calls=%async_computation.10 | async-start | bytes 2924544 | tf_op jit(solution)/shard_map/reduce_scatter | solution.py:35
  22.3 1.2 copy-start.3
  28.1 2.9 copy-start.9
  28.1 244.0 %reduce-scatter.18.cloned.1.call-start = ((), (), s32[]{:S(2)}) async-start(), calls=%async_computation.11 | async-start | bytes 2924544 | tf_op jit(solution)/shard_map/reduce_scatter | solution.py:38
  31.9 1.2 copy-start.4
  37.7 308.6 %all-gather.5.cloned.1.call-start = ((), (), s32[]{:S(2)}) async-start(), calls=%async_computation.8 | async-start | bytes 2924544 | tf_op jit(solution)/shard_map/all_gather | solution.py:65
  274.2 125.2 %all-gather.3.cloned.1.call-start = ((), (), s32[]{:S(2)}) async-start(), calls=%async_computation.6 | async-start | bytes 2924544 | tf_op jit(solution)/shard_map/all_gather | solution.py:45
  276.5 41.2 %all-to-all-start = ((bf16[16,48,1792]{2,1,0:T(8,128)(2,1)}), bf16[16,48,1792]{2,1,0:T(8,128)(2,1)S(1)}, u32[]{:S(2)}, u32[]{:S(2)}) async-start(bf16[16,48,1792]{2,1,0:T(8,128)(2,1)} %stack.2), calls=%async_computation.1 | async-start | bytes 5505024 | tf_op jit(solution)/shard_map/all_to_all | solution.py:63
  282.2 163.5 %all-reduce.3.cloned.1.call-start = ((), (), s32[]{:S(2)}) async-start(), calls=%async_computation.13 | async-start | bytes 11010048 | tf_op jit(solution)/shard_map/psum | solution.py:76
  399.4 2.2 copy-start.10
  399.4 2.2 copy-start.13
  404.5 84.0 %reduce-scatter.12.cloned.1.call-start = ((), (), s32[]{:S(2)}) async-start(), calls=%async_computation.7 | async-start | bytes 884736 | tf_op jit(solution)/shard_map/reduce_scatter | solution.py:46
  410.0 118.6 %reduce-scatter.14.cloned.1.call-start = ((), (), s32[]{:S(2)}) async-start(), calls=%async_computation.9 | async-start | bytes 884736 | tf_op jit(solution)/shard_map/reduce_scatter | solution.py:67
  410.0 3.3 copy-start.2
  410.0 3.3 copy-start.5
  449.5 79.1 %copy-start.6 = (bf16[1792,512]{1,0:T(8,128)(2,1)S(1)}, bf16[1792,512]{1,0:T(8,128)(2,1)}, u32[]{:S(2)}) copy-start(bf16[1792,512]{1,0:T(8,128)(2,1)} %get-tuple-element.41) | copy-start | bytes 5505028
  528.6 1.7 copy-start.1
Sparse Core Ops, SparseCore 0:
  19.2 84.0 reduce-scatter.19
  106.9 80.7 reduce-scatter.15
  191.3 80.7 reduce-scatter.17
  274.4 71.7 all-gather.4
  348.6 50.6 all-gather.2
  404.6 41.0 all-reduce.2
  448.8 39.6 reduce-scatter.11
  491.6 36.9 reduce-scatter.13
